TPU v7x, 256 devices: a whole 4x4x8 slice. The times are simulated.
256 devices in a mesh: row: 32 (over y, z), col: 8 (over x, core).
Axes of the slice: x: 4, y: 4, z: 8, core: 2. Of those that a mesh axis runs over, the one named last changes fastest.
Arguments:
- panel: float32 [8, 32, 256, 256], P(None, 'row', None, 'col'), may hold values from -0.1875 to 0.1875
- slab: bfloat16 [8, 32, 256, 4, 8, 256], P(None, 'row', None, None, 'col'), may hold values from -6 to 6
- cotangent: bfloat16 [8, 32, 256, 4, 8, 256], P(None, 'row', None, None, 'col'), may hold values from -0.0625 to 0.0625
- inverse: float32 [256, 256], replicated, may hold values from -2 to 8, as said below
Outputs:
- updated: bfloat16 [8, 32, 256, 4, 8, 256], P(None, 'row', None, None, 'col')
- grad_panel: float32 [8, 32, 256, 256], P(None, 'row', None, 'col')
- grad_inverse: float32 [256, 256], P(None, 'col')
Inputs may be any that keep to these rules, and one draw needn't show every extreme that they name: `inverse`: lower triangular; diagonal entries between 4 and 8.
All inputs are finite; a program needn't handle non-finite values.
Results may differ from a plain program's by a relative error of at most 0.015.
Values may be sent and summed in bfloat16 or wider, within the bound.
A program may use at most 128 MiB of HBM per device.

v0:
```python
import jax
import jax.numpy as jnp
from jax import lax
from jax.sharding import PartitionSpec as P


def per_device(panel, slab, cotangent, inverse):
    tiles_local = panel.shape[0]
    tile_size = panel.shape[2]
    strip_width = panel.shape[3]
    slab_tiles = slab.shape[3]
    row_count = tiles_local * tile_size
    slab_width = slab_tiles * tile_size
    row_devices = lax.axis_size("row")
    col_devices = lax.axis_size("col")
    row_index = lax.axis_index("row")
    col_index = lax.axis_index("col")
    highest = lax.Precision.HIGHEST
    contract_rows = (((0,), (0,)), ((), ()))
    panel_rows = panel.reshape(row_count, strip_width)
    gathered = lax.all_gather(panel_rows, "col", axis=1, tiled=True)
    factor = jnp.dot(gathered, inverse.T, precision=highest, preferred_element_type=jnp.float32)
    rounded = factor.astype(jnp.bfloat16)
    factor_tiles = rounded.reshape(tiles_local, tile_size, tile_size)
    tile_list = []
    for column_slot in range(slab_tiles):
        tile_index = column_slot * col_devices + col_index
        is_owner = tile_index % row_devices == row_index
        owned_tile = lax.dynamic_index_in_dim(
            factor_tiles, tile_index // row_devices, 0, keepdims=False
        )
        tile_list.append(jnp.where(is_owner, owned_tile, jnp.zeros_like(owned_tile)))
    stacked = jnp.stack(tile_list).reshape(slab_width, tile_size)
    slab_factor = lax.psum(stacked, "row").astype(jnp.float32).astype(jnp.bfloat16)
    slab_rows = slab.reshape(row_count, slab_width)
    product = jnp.dot(rounded, slab_factor.T, preferred_element_type=jnp.float32)
    updated = (slab_rows.astype(jnp.float32) - product).astype(jnp.bfloat16)
    cot_rows = cotangent.reshape(row_count, slab_width)
    factor_grad = -jnp.dot(cot_rows, slab_factor, preferred_element_type=jnp.float32)
    slab_grad = -lax.dot_general(
        cot_rows, rounded, contract_rows, preferred_element_type=jnp.float32
    )
    slab_grad = lax.psum(slab_grad.astype(jnp.bfloat16), "row").astype(jnp.float32)
    grad_tiles = factor_grad.reshape(tiles_local, tile_size, tile_size)
    for column_slot in range(slab_tiles):
        tile_index = column_slot * col_devices + col_index
        is_owner = tile_index % row_devices == row_index
        local_slot = tile_index // row_devices
        current_tile = lax.dynamic_index_in_dim(grad_tiles, local_slot, 0, keepdims=True)
        added_tile = jnp.where(
            is_owner, slab_grad[column_slot * tile_size : (column_slot + 1) * tile_size], 0.0
        )
        grad_tiles = lax.dynamic_update_index_in_dim(
            grad_tiles, current_tile + added_tile[None], local_slot, 0
        )
    factor_grad = grad_tiles.reshape(row_count, tile_size)
    grad_total = lax.psum(factor_grad, "col")
    inverse_strip = lax.dynamic_slice_in_dim(inverse, col_index * strip_width, strip_width, 1)
    grad_panel = jnp.dot(
        grad_total, inverse_strip, precision=highest, preferred_element_type=jnp.float32
    )
    inverse_term = lax.dot_general(
        grad_total, panel_rows, contract_rows, precision=highest, preferred_element_type=jnp.float32
    )
    grad_inverse = lax.psum(inverse_term, "row")
    return (updated.reshape(slab.shape), grad_panel.reshape(panel.shape), grad_inverse)


def solution(mesh):
    in_specs = (
        P(None, "row", None, "col"),
        P(None, "row", None, None, "col", None),
        P(None, "row", None, None, "col", None),
        P(),
    )
    out_specs = (
        P(None, "row", None, None, "col", None),
        P(None, "row", None, "col"),
        P(None, "col"),
    )
    return jax.shard_map(
        per_device, mesh=mesh, in_specs=in_specs, out_specs=out_specs, check_vma=False
    )
```

profile of v0, /device:TPU:0, one launch (start us, length us, event | category | flops | bytes accessed | tf_op | source)
XLA Modules:
  0.0 430.0 jit_solution(7106329265095890)
XLA Ops:
  7.2 1.7 copy.19
  9.1 5.2 %copy.20 = bf16[256,8,4,256]{3,1,2,0:T(8,128)(2,1)} copy(bf16[256,8,4,256]{3,2,1,0:T(4,128)(2,1)} %bitcast.71) | data formatting | bytes 8388608
  14.3 24.5 %all-gather.2.cloned.1.call-done = f32[2048,256]{0,1:T(8,128)} async-done(((f32[2048,32]{0,1:T(8,128)}), f32[2048,256]{0,1:T(8,128)}) %all-gather.2.cloned.1.call-update) | async-done | bytes 2097168 | tf_op jit(solution)/shard_map/all_gather | solution.py:21
  38.8 5.0 %convolution_convert_fusion = bf16[2048,256]{1,0:T(8,128)(2,1)S(1)} fusion(f32[2048,256]{0,1:T(8,128)} %all-gather.2.cloned.1.call-done, f32[256,256]{1,0:T(8,128)S(1)} %copy-done), kind=kOutput, calls=%fused_computation.2 | convolution fusion | flops 1611137024 | bytes 3407872 | tf_op jit(solution)/shard_map/dot_general | solution.py:22
  43.9 4.3 fusion.1
  48.2 0.9 pad_maximum_fusion
  49.1 0.2 all-reduce.4.cloned.1.call-start
  49.3 150.0 %all-reduce.6.cloned.1.call-done = (bf16[1024,256]{1,0:T(8,128)(2,1)}, bf16[1024,256]{0,1:T(8,128)(2,1)}) async-done(((bf16[1024,256]{1,0:T(8,128)(2,1)}, bf16[1024,256]{0,1:T(8,128)(2,1)}), (bf16[1024,256]{1,0:T(8,128)(2,1)}, bf16[1024,256]{0,1:T(8,128)(2,1)})) %all-reduce.6.cloned.1.call-update) | async-done | bytes 1048592 | tf_op jit(solution)/shard_map/psum | solution.py:34
  199.3 3.7 convolution_negate_fusion
  202.9 0.2 copy.24
  203.1 0.9 copy-done.4
  204.0 0.1 convert_element_type.29
  204.1 0.1 fusion.13
  204.2 0.1 fusion.7
  204.4 1.8 copy.14
  206.2 7.0 %copy.18 = f32[256,8,4,256]{3,1,2,0:T(8,128)} copy(bf16[256,8,4,256]{3,2,1,0:T(4,128)(2,1)} %bitcast.70) | data formatting | bytes 12582912
  213.2 6.8 %subtract_convert_fusion = bf16[2048,1024]{1,0:T(8,128)(2,1)} fusion(f32[2048,1024]{1,0:T(8,128)} %bitcast.66, bf16[2048,256]{1,0:T(8,128)(2,1)S(1)} %convolution_convert_fusion, bf16[1024,256]{1,0:T(8,128)(2,1)S(1)} %copy-done.3), kind=kOutput, calls=%fused_computation | convolution fusion | flops 1077936128 | bytes 14155776 | tf_op jit(solution)/shard_map/dot_general | solution.py:36
  220.1 7.9 %reshape.36 = bf16[8,1,256,4,1,256]{5,3,2,0,4,1:T(4,128)(2,1)} reshape(bf16[2048,1024]{1,0:T(8,128)(2,1)} %subtract_convert_fusion) | data formatting | bytes 8388608 | tf_op jit(solution)/shard_map/reshape | solution.py:66
  227.9 46.6 %all-reduce.4.cloned.1.call-done = f32[2048,256]{1,0:T(8,128)} async-done(((f32[2048,256]{1,0:T(8,128)}), f32[2048,256]{1,0:T(8,128)}) %all-reduce.4.cloned.1.call-update) | async-done | bytes 2097168 | tf_op jit(solution)/shard_map/psum | solution.py:57
  274.5 3.8 fusion.14
  278.3 0.1 copy.21
  278.4 0.8 copy.16
  279.2 1.2 fusion.17
  280.4 143.1 %psum.31 = f32[256,32]{0,1:T(8,128)} all-reduce(f32[256,32]{0,1:T(8,128)S(1)} %fusion.17), channel_id=1, replica_groups=mesh['row'=32,'col'=8] {'row'}, use_global_device_ids=true, to_apply=%region_3.4 | all-reduce | flops 8192 | bytes 65536 | tf_op jit(solution)/shard_map/psum | solution.py:65
  (17 shorter events, 0.3 us)
Async XLA Ops:
  7.2 31.7 %copy-start = (f32[256,256]{1,0:T(8,128)S(1)}, f32[256,256]{1,0:T(8,128)}, u32[]{:S(2)}) copy-start(f32[256,256]{1,0:T(8,128)} %param.7) | copy-start | bytes 786436
  7.2 31.7 %all-gather.2.cloned.1.call-start = ((), (), s32[]{:S(2)}) async-start(), calls=%async_computation | async-start | bytes 2359296 | tf_op jit(solution)/shard_map/all_gather | solution.py:21
  9.0 190.3 %all-reduce.6.cloned.1.call-start = ((), (), s32[]{:S(2)}) async-start(), calls=%async_computation.2 | async-start | bytes 2097152 | tf_op jit(solution)/shard_map/psum | solution.py:34
  49.1 225.4 %all-reduce.4.cloned.1.call-start = ((), (), s32[]{:S(2)}) async-start(), calls=%async_computation.1 | async-start | bytes 4194304 | tf_op jit(solution)/shard_map/psum | solution.py:57
  202.9 1.0 copy-start.4
  206.2 7.0 %copy-start.3 = (bf16[1024,256]{1,0:T(8,128)(2,1)S(1)}, bf16[1024,256]{1,0:T(8,128)(2,1)}, u32[]{:S(2)}) copy-start(bf16[1024,256]{1,0:T(8,128)(2,1)} %get-tuple-element.9) | copy-start | bytes 1572868
  227.9 51.3 %copy-start.2 = (f32[4,8,8,256]{3,1,2,0:T(8,128)S(1)}, f32[4,8,8,256]{3,1,2,0:T(8,128)}, u32[]{:S(2)}) copy-start(f32[4,8,8,256]{3,1,2,0:T(8,128)} %copy.19) | copy-start | bytes 786436
  274.5 4.7 %copy-start.1 = (f32[2048,256]{1,0:T(8,128)S(1)}, f32[2048,256]{1,0:T(8,128)}, u32[]{:S(2)}) copy-start(f32[2048,256]{1,0:T(8,128)} %all-reduce.4.cloned.1.call-done) | copy-start | bytes 6291460
Sparse Core Ops, SparseCore 0:
  9.9 28.9 all-gather.1
  49.2 150.0 all-reduce.5
  206.3 68.1 all-reduce.3
where the time goes:
time: 431 us; the launch traced here: 430 us
  waiting for transfers between devices  221 us (51%)
  blocking collectives  143 us (33%)
  local copies, waits for them, and re-layouts  25.5 us (6%)
  matrix products  24.8 us (6%)
  between operations  13.9 us (3%)
    psum x1, waiting for transfers between devices, per_device(): lax.psum(stacked, 'row').astype(jnp.float32).astype(jnp.bfloat16)  150 us
    psum x1, blocking collectives, per_device(): grad_inverse = lax.psum(inverse_term, 'row')  143 us
    psum x1, waiting for transfers between devices, per_device(): grad_total = lax.psum(factor_grad, 'col')  46.6 us
    all_gather x1, waiting for transfers between devices, per_device(): gathered = lax.all_gather(panel_rows, 'col', axis=1, tiled=True)  24.5 us
    unnamed x15, local copies, waits for them, and re-layouts  15.7 us
  transfers between devices with their start and end apart: 3, of which 3 were waited for; matrix products, arithmetic and copies ran while one was open for 6% of the time, Pallas kernels for 0%

commit v1 on v0

--- a/solution.py
+++ b/solution.py
@@ -54,7 +54,7 @@
             grad_tiles, current_tile + added_tile[None], local_slot, 0
         )
     factor_grad = grad_tiles.reshape(row_count, tile_size)
-    grad_total = lax.psum(factor_grad, "col")
+    grad_total = jnp.sum(lax.all_gather(factor_grad, "col"), axis=0)
     inverse_strip = lax.dynamic_slice_in_dim(inverse, col_index * strip_width, strip_width, 1)
     grad_panel = jnp.dot(
         grad_total, inverse_strip, precision=highest, preferred_element_type=jnp.float32

time: 431 us -> 455 us (1.056)
  waiting for transfers between devices: 221 us -> 237 us
  other arithmetic: 1.27 us -> 8.4 us
    all_gather x0 -> x1, waiting for transfers between devices: none -> 62.4 us  [per_device(): grad_total = jnp.sum(lax.all_gather(factor_grad, 'col'), axis=0)]
    psum x1 -> x0, waiting for transfers between devices: 46.6 us -> none  [per_device(): grad_total = lax.psum(factor_grad, 'col')]
    reduce_sum x0 -> x1, other arithmetic: none -> 7.14 us  [per_device(): grad_total = jnp.sum(lax.all_gather(factor_grad, 'col'), axis=0)]
    unnamed x15 -> x11, local copies, waits for them, and re-layouts: 15.7 us -> 14.8 us
where the time goes in v1:
time: 455 us; the launch traced here: 453 us
  waiting for transfers between devices  237 us (52%)
  blocking collectives  143 us (31%)
  local copies, waits for them, and re-layouts  24.8 us (5%)
  matrix products  24.5 us (5%)
  between operations  13.9 us (3%)
  other arithmetic  8.4 us (2%)
    psum x1, waiting for transfers between devices, per_device(): lax.psum(stacked, 'row').astype(jnp.float32).astype(jnp.bfloat16)  150 us
    psum x1, blocking collectives, per_device(): grad_inverse = lax.psum(inverse_term, 'row')  143 us
    all_gather x1, waiting for transfers between devices, per_device(): grad_total = jnp.sum(lax.all_gather(factor_grad, 'col'), axis=0)  62.4 us
    all_gather x1, waiting for transfers between devices, per_device(): gathered = lax.all_gather(panel_rows, 'col', axis=1, tiled=True)  25.1 us
    unnamed x11, local copies, waits for them, and re-layouts  14.8 us
  transfers between devices with their start and end apart: 3, of which 3 were waited for; matrix products, arithmetic and copies ran while one was open for 6% of the time, Pallas kernels for 0%

profile of v1, /device:TPU:0, one launch (start us, length us, event | category | flops | bytes accessed | tf_op | source)
XLA Modules:
  0.0 452.6 jit_solution(4560713553950819846)
XLA Ops:
  7.2 1.7 copy.29
  9.1 5.2 %copy.30 = bf16[256,8,4,256]{3,1,2,0:T(8,128)(2,1)} copy(bf16[256,8,4,256]{3,2,1,0:T(4,128)(2,1)} %bitcast.76) | data formatting | bytes 8388608
  14.3 25.1 %all-gather.3.cloned.1.call-done = f32[2048,256]{0,1:T(8,128)} async-done(((f32[2048,32]{0,1:T(8,128)}), f32[2048,256]{0,1:T(8,128)}) %all-gather.3.cloned.1.call-update) | async-done | bytes 2097168 | tf_op jit(solution)/shard_map/all_gather | solution.py:21
  39.4 5.0 %convolution_convert_fusion = bf16[2048,256]{1,0:T(8,128)(2,1)S(1)} fusion(f32[2048,256]{0,1:T(8,128)} %all-gather.3.cloned.1.call-done, f32[256,256]{1,0:T(8,128)S(1)} %copy-done), kind=kOutput, calls=%fused_computation.2 | convolution fusion | flops 1611137024 | bytes 3407872 | tf_op jit(solution)/shard_map/dot_general | solution.py:22
  44.4 4.3 fusion.1
  48.8 0.9 pad_maximum_fusion
  49.7 0.2 all-gather.5.cloned.1.call-start
  49.9 150.0 %all-reduce.3.cloned.1.call-done = (bf16[1024,256]{1,0:T(8,128)(2,1)}, bf16[1024,256]{0,1:T(8,128)(2,1)}) async-done(((bf16[1024,256]{1,0:T(8,128)(2,1)}, bf16[1024,256]{0,1:T(8,128)(2,1)}), (bf16[1024,256]{1,0:T(8,128)(2,1)}, bf16[1024,256]{0,1:T(8,128)(2,1)})) %all-reduce.3.cloned.1.call-update) | async-done | bytes 1048592 | tf_op jit(solution)/shard_map/psum | solution.py:34
  199.9 3.7 convolution_negate_fusion
  203.6 0.2 copy.33
  203.7 0.9 copy-done.3
  204.6 0.1 convert_element_type.29
  204.7 0.1 fusion.13
  204.8 0.1 fusion.10
  204.8 0.1 fusion.7
  205.0 1.8 copy.22
  206.8 7.0 %copy.28 = f32[256,8,4,256]{3,1,2,0:T(8,128)} copy(bf16[256,8,4,256]{3,2,1,0:T(4,128)(2,1)} %bitcast.75) | data formatting | bytes 12582912
  213.8 7.6 %subtract_convert_fusion = bf16[2048,1024]{1,0:T(8,128)(2,1)} fusion(f32[2048,1024]{1,0:T(8,128)} %bitcast.70, bf16[2048,256]{1,0:T(8,128)(2,1)S(1)} %convolution_convert_fusion, bf16[1024,256]{1,0:T(8,128)(2,1)S(1)} %copy-done.2), kind=kOutput, calls=%fused_computation | convolution fusion | flops 1077936128 | bytes 14155776 | tf_op jit(solution)/shard_map/dot_general | solution.py:36
  221.4 8.0 %reshape.37 = bf16[8,1,256,4,1,256]{5,3,2,0,4,1:T(4,128)(2,1)} reshape(bf16[2048,1024]{1,0:T(8,128)(2,1)} %subtract_convert_fusion) | data formatting | bytes 8388608 | tf_op jit(solution)/shard_map/reshape | solution.py:66
  229.4 62.4 %all-gather.5.cloned.1.call-done = f32[8,2048,256]{2,1,0:T(8,128)} async-done(((f32[1,2048,256]{2,1,0:T(8,128)}), f32[8,2048,256]{2,1,0:T(8,128)}) %all-gather.5.cloned.1.call-update) | async-done | bytes 16777232 | tf_op jit(solution)/shard_map/all_gather | solution.py:57
  291.8 7.1 %reduce_sum.9 = f32[2048,256]{1,0:T(8,128)S(1)} reduce(f32[8,2048,256]{2,1,0:T(8,128)} %all-gather.5.cloned.1.call-done, f32[]{:T(128)} %constant.125.clone.1), dimensions={0}, to_apply=%region_2.3 | reduce | flops 3670016 | bytes 18874372 | tf_op jit(solution)/shard_map/reduce_sum | solution.py:57
  298.9 1.2 fusion.17
  300.1 143.2 %psum.23 = f32[256,32]{0,1:T(8,128)} all-reduce(f32[256,32]{0,1:T(8,128)S(1)} %fusion.17), channel_id=1, replica_groups=mesh['row'=32,'col'=8] {'row'}, use_global_device_ids=true, to_apply=%region_3.4 | all-reduce | flops 8192 | bytes 65536 | tf_op jit(solution)/shard_map/psum | solution.py:65
  443.3 2.8 convolution_bitcast_fusion
  (14 shorter events, 0.3 us)
Async XLA Ops:
  7.2 32.2 %copy-start = (f32[256,256]{1,0:T(8,128)S(1)}, f32[256,256]{1,0:T(8,128)}, u32[]{:S(2)}) copy-start(f32[256,256]{1,0:T(8,128)} %param.7) | copy-start | bytes 786436
  7.2 32.2 %all-gather.3.cloned.1.call-start = ((), (), s32[]{:S(2)}) async-start(), calls=%async_computation | async-start | bytes 2359296 | tf_op jit(solution)/shard_map/all_gather | solution.py:21
  9.0 190.9 %all-reduce.3.cloned.1.call-start = ((), (), s32[]{:S(2)}) async-start(), calls=%async_computation.2 | async-start | bytes 2097152 | tf_op jit(solution)/shard_map/psum | solution.py:34
  49.7 242.1 %all-gather.5.cloned.1.call-start = ((), (), s32[]{:S(2)}) async-start(), calls=%async_computation.1 | async-start | bytes 18874368 | tf_op jit(solution)/shard_map/all_gather | solution.py:57
  203.5 1.0 copy-start.3
  206.8 7.0 %copy-start.2 = (bf16[1024,256]{1,0:T(8,128)(2,1)S(1)}, bf16[1024,256]{1,0:T(8,128)(2,1)}, u32[]{:S(2)}) copy-start(bf16[1024,256]{1,0:T(8,128)(2,1)} %get-tuple-element.12) | copy-start | bytes 1572868
  229.4 69.5 %copy-start.1 = (f32[4,8,8,256]{3,1,2,0:T(8,128)S(1)}, f32[4,8,8,256]{3,1,2,0:T(8,128)}, u32[]{:S(2)}) copy-start(f32[4,8,8,256]{3,1,2,0:T(8,128)} %copy.29) | copy-start | bytes 786436
Sparse Core Ops, SparseCore 0:
  10.4 28.9 all-gather.2
  49.8 150.0 all-reduce.2
  207.0 84.7 all-gather.4
